TPU v7x, 256 devices: a whole 4x4x8 slice. The times are simulated.
256 devices in a mesh: row: 16 (over z, core), col: 16 (over y, x).
Axes of the slice: x: 4, y: 4, z: 8, core: 2. Of those that a mesh axis runs over, the one named last changes fastest.
Arguments:
- rhs: float32 [24576, 12288], P('row', 'col'), may hold values from -6 to 6
- panels_l: float32 [4, 24576, 512], P(None, 'row', 'col'), may hold values from -0.25 to 0.25
- diag_inverse: float32 [4, 512, 512], P(None, None, 'col'), may hold values from -1.5 to 1.5, as said below
Outputs:
- solved_rhs: float32 [24576, 12288], P('row', 'col')
Inputs may be any that keep to these rules, and one draw needn't show every extreme that they name: `diag_inverse`: each tile is lower triangular with diagonal entries between 0.5 and 1.5.
All inputs are finite; a program needn't handle non-finite values.
Results may differ from a plain program's by a relative error of at most 0.00016.
Values sent between devices are 32-bit elements; how exact they have to be, the bound alone decides.
A program may use at most 128 MiB of HBM per device.

v0:
```python
import jax
import jax.numpy as jnp
from jax import lax
from jax.sharding import PartitionSpec as P


def spread(x, axis, root):
    mine = lax.axis_index(axis) == root
    return lax.psum(jnp.where(mine, x, jnp.zeros_like(x)), axis)


def exact_dot(left, right):
    return jnp.dot(left, right, precision=lax.Precision.HIGHEST, preferred_element_type=jnp.float32)


def per_device(rhs, panels_l, diag_inverse):
    rows_here = rhs.shape[0]
    width = diag_inverse.shape[1]
    count = panels_l.shape[0]
    my_row = lax.axis_index("row")
    global_rows = my_row * rows_here + lax.iota(jnp.int32, rows_here)
    work = rhs
    for k in range(count):
        factor_cols = lax.all_gather(panels_l[k], "col", axis=1, tiled=True)
        inverse_tile = lax.all_gather(diag_inverse[k], "col", axis=1, tiled=True)
        owner = k * width // rows_here
        offset = k * width - owner * rows_here
        strip = work[offset : offset + width]
        is_owner = my_row == owner
        solved_here = lax.cond(
            is_owner,
            lambda: exact_dot(inverse_tile, strip),
            lambda: jnp.zeros(strip.shape, jnp.float32),
        )
        solved = spread(solved_here, "row", owner)
        update = exact_dot(factor_cols, solved)
        below = (global_rows >= (k + 1) * width)[:, None]
        work = jnp.where(below, work - update, work)
        work = work.at[offset : offset + width].set(
            jnp.where(is_owner, solved, work[offset : offset + width])
        )
    return work


def solution(mesh):
    in_specs = (P("row", "col"), P(None, "row", "col"), P(None, None, "col"))
    out_specs = P("row", "col")
    return jax.shard_map(
        per_device, mesh=mesh, in_specs=in_specs, out_specs=out_specs, check_vma=False
    )
```

profile of v0, /device:TPU:32, one launch (start us, length us, event | category | flops | bytes accessed | tf_op | source)
XLA Modules:
  0.0 915.7 jit_solution(2855108133627082533)
XLA Ops:
  6.5 1.0 fusion.27
  7.5 0.7 copy.52
  8.3 51.6 %all-gather.17.cloned.1.call-done = f32[1,512,512]{1,0,2:T(1,128)} async-done(((f32[1,512,32]{1,0,2:T(1,128)}), f32[1,512,512]{1,0,2:T(1,128)}) %all-gather.17.cloned.1.call-update) | async-done | bytes 1048592 | tf_op jit(solution)/shard_map/all_gather | solution.py:25
  59.9 1.3 copy.69
  61.2 0.2 conditional.4
  61.2 0.2 broadcast.87.clone
  61.4 1.4 broadcast_select_fusion.3
  62.8 1.1 copy-done.7
  63.9 0.9 fusion.26
  64.8 0.0 all-gather.21.cloned.1.call-start
  64.9 0.7 copy.53
  65.6 0.5 all-gather.23.cloned.1.call-update
  66.2 6.0 copy.21
  72.3 101.1 %all-reduce.5.cloned.1.call-done = f32[512,768]{0,1:T(8,128)} async-done(((f32[512,768]{0,1:T(8,128)}), f32[512,768]{0,1:T(8,128)}) %all-reduce.5.cloned.1.call-update) | async-done | bytes 1572880 | tf_op jit(solution)/shard_map/psum | solution.py:9
  173.4 58.4 %all-gather.19.cloned.1.call-done = f32[1,1536,512]{1,2,0:T(8,128)} async-done(((f32[1,1536,32]{1,2,0:T(8,128)}), f32[1,1536,512]{1,2,0:T(8,128)}) %all-gather.19.cloned.1.call-update) | async-done | bytes 3145744 | tf_op jit(solution)/shard_map/all_gather | solution.py:24
  231.8 12.0 %subtract_select_fusion.3 = f32[1536,768]{0,1:T(8,128)} fusion(f32[1536,768]{0,1:T(8,128)} %copy.21, f32[512,768]{0,1:T(8,128)} %all-reduce.5.cloned.1.call-done, f32[1,1536,512]{1,2,0:T(8,128)} %all-gather.19.cloned.1.call-done, pred[1536]{0:T(1024)(128)(4,1)S(1)} %fusion.22), kind=kOutput, calls=%fused_computation.17 | convolution fusion | flops 7250116608 | bytes 14157312 | tf_op jit(solution)/shard_map/dot_general | solution.py:13
  243.8 2.9 fusion.21
  246.7 33.7 %all-gather.21.cloned.1.call-done = f32[1,512,512]{1,0,2:T(1,128)} async-done(((f32[1,512,32]{1,0,2:T(1,128)}), f32[1,512,512]{1,0,2:T(1,128)}) %all-gather.21.cloned.1.call-update) | async-done | bytes 1048592 | tf_op jit(solution)/shard_map/all_gather | solution.py:25
  280.4 0.4 conditional.5
  280.4 0.2 broadcast.88.clone
  280.8 1.3 broadcast_select_fusion.2
  282.1 0.0 all-gather.25.cloned.1.call-start
  282.2 0.7 copy.54
  282.9 0.7 all-gather.27.cloned.1.call-update
  283.7 51.2 %all-gather.23.cloned.1.call-done = f32[1,1536,512]{1,2,0:T(8,128)} async-done(((f32[1,1536,32]{1,2,0:T(8,128)}), f32[1,1536,512]{1,2,0:T(8,128)}) %all-gather.23.cloned.1.call-update) | async-done | bytes 3145744 | tf_op jit(solution)/shard_map/all_gather | solution.py:24
  334.9 112.1 %all-reduce.7.cloned.1.call-done = f32[512,768]{0,1:T(8,128)} async-done(((f32[512,768]{0,1:T(8,128)}), f32[512,768]{0,1:T(8,128)}) %all-reduce.7.cloned.1.call-update) | async-done | bytes 1572880 | tf_op jit(solution)/shard_map/psum | solution.py:9
  447.0 12.9 %subtract_select_fusion.2 = f32[1536,768]{0,1:T(8,128)} fusion(f32[1536,768]{0,1:T(8,128)} %fusion.21, f32[512,768]{0,1:T(8,128)} %all-reduce.7.cloned.1.call-done, f32[1,1536,512]{1,2,0:T(8,128)} %all-gather.23.cloned.1.call-done, pred[1536]{0:T(1024)(128)(4,1)S(1)} %fusion.23), kind=kOutput, calls=%fused_computation.16 | convolution fusion | flops 7250116608 | bytes 14157312 | tf_op jit(solution)/shard_map/dot_general | solution.py:13
  459.9 2.9 fusion.20
  462.8 37.3 %all-gather.25.cloned.1.call-done = f32[1,512,512]{1,0,2:T(1,128)} async-done(((f32[1,512,32]{1,0,2:T(1,128)}), f32[1,512,512]{1,0,2:T(1,128)}) %all-gather.25.cloned.1.call-update) | async-done | bytes 1048592 | tf_op jit(solution)/shard_map/all_gather | solution.py:25
  500.1 0.2 conditional.6
  500.1 0.2 broadcast.89.clone
  500.3 1.3 broadcast_select_fusion.1
  501.7 0.7 copy.55
  502.5 0.7 all-gather.31.cloned.1.call-update
  503.1 0.3 all-reduce.11.cloned.1.call-start
  503.4 51.3 %all-gather.27.cloned.1.call-done = f32[1,1536,512]{1,2,0:T(8,128)} async-done(((f32[1,1536,32]{1,2,0:T(8,128)}), f32[1,1536,512]{1,2,0:T(8,128)}) %all-gather.27.cloned.1.call-update) | async-done | bytes 3145744 | tf_op jit(solution)/shard_map/all_gather | solution.py:24
  554.8 112.3 %all-reduce.9.cloned.1.call-done = f32[512,768]{0,1:T(8,128)} async-done(((f32[512,768]{0,1:T(8,128)}), f32[512,768]{0,1:T(8,128)}) %all-reduce.9.cloned.1.call-update) | async-done | bytes 1572880 | tf_op jit(solution)/shard_map/psum | solution.py:9
  667.0 12.9 %subtract_select_fusion.1 = f32[1536,768]{0,1:T(8,128)} fusion(f32[1536,768]{0,1:T(8,128)} %fusion.20, f32[512,768]{0,1:T(8,128)} %all-reduce.9.cloned.1.call-done, f32[1,1536,512]{1,2,0:T(8,128)} %all-gather.27.cloned.1.call-done, pred[1536]{0:T(1024)(128)(4,1)S(1)} %fusion.24), kind=kOutput, calls=%fused_computation.15 | convolution fusion | flops 7250116608 | bytes 14157312 | tf_op jit(solution)/shard_map/dot_general | solution.py:13
  680.0 2.9 fusion.19
  682.9 37.1 %all-gather.29.cloned.1.call-done = f32[1,512,512]{1,0,2:T(1,128)} async-done(((f32[1,512,32]{1,0,2:T(1,128)}), f32[1,512,512]{1,0,2:T(1,128)}) %all-gather.29.cloned.1.call-update) | async-done | bytes 1048592 | tf_op jit(solution)/shard_map/all_gather | solution.py:25
  719.9 0.5 conditional.7
  719.9 0.2 broadcast.90.clone
  720.4 1.3 broadcast_select_fusion
  721.8 52.8 %all-gather.31.cloned.1.call-done = f32[1,1536,512]{1,2,0:T(8,128)} async-done(((f32[1,1536,32]{1,2,0:T(8,128)}), f32[1,1536,512]{1,2,0:T(8,128)}) %all-gather.31.cloned.1.call-update) | async-done | bytes 3145744 | tf_op jit(solution)/shard_map/all_gather | solution.py:24
  774.6 112.1 %all-reduce.11.cloned.1.call-done = f32[512,768]{0,1:T(8,128)} async-done(((f32[512,768]{0,1:T(8,128)}), f32[512,768]{0,1:T(8,128)}) %all-reduce.11.cloned.1.call-update) | async-done | bytes 1572880 | tf_op jit(solution)/shard_map/psum | solution.py:9
  886.8 13.1 %subtract_select_fusion = f32[1536,768]{0,1:T(8,128)} fusion(f32[1536,768]{0,1:T(8,128)} %fusion.19, f32[512,768]{0,1:T(8,128)} %all-reduce.11.cloned.1.call-done, f32[1,1536,512]{1,2,0:T(8,128)} %all-gather.31.cloned.1.call-done, pred[1536]{0:T(1024)(128)(4,1)S(1)} %fusion.25), kind=kOutput, calls=%fused_computation.14 | convolution fusion | flops 7250116608 | bytes 14157312 | tf_op jit(solution)/shard_map/dot_general | solution.py:13
  899.8 3.0 fusion.18
  902.8 6.0 copy.35
  (31 shorter events, 0.5 us)
Async XLA Ops:
  6.5 53.3 %all-gather.17.cloned.1.call-start = ((), (), s32[]{:S(2)}) async-start(), calls=%async_computation.4 | async-start | bytes 1114112 | tf_op jit(solution)/shard_map/all_gather | solution.py:25
  8.2 165.2 %all-reduce.5.cloned.1.call-start = ((), (), s32[]{:S(2)}) async-start(), calls=%async_computation | async-start | bytes 3145728 | tf_op jit(solution)/shard_map/psum | solution.py:9
  62.7 1.1 copy-start.7
  62.8 169.0 %all-gather.19.cloned.1.call-start = ((), (), s32[]{:S(2)}) async-start(), calls=%async_computation.5 | async-start | bytes 3342336 | tf_op jit(solution)/shard_map/all_gather | solution.py:24
  64.8 215.6 %all-gather.21.cloned.1.call-start = ((), (), s32[]{:S(2)}) async-start(), calls=%async_computation.6 | async-start | bytes 1114112 | tf_op jit(solution)/shard_map/all_gather | solution.py:25
  65.6 269.3 %all-gather.23.cloned.1.call-start = ((), (), s32[]{:S(2)}) async-start(), calls=%async_computation.7 | async-start | bytes 3342336 | tf_op jit(solution)/shard_map/all_gather | solution.py:24
  66.2 380.9 %all-reduce.7.cloned.1.call-start = ((), (), s32[]{:S(2)}) async-start(), calls=%async_computation.1 | async-start | bytes 3145728 | tf_op jit(solution)/shard_map/psum | solution.py:9
  173.4 70.4 %copy-start = (f32[512,768]{0,1:T(8,128)S(1)}, f32[512,768]{0,1:T(8,128)}, u32[]{:S(2)}) copy-start(f32[512,768]{0,1:T(8,128)} %all-reduce.5.cloned.1.call-done) | copy-start | bytes 4718596
  282.1 218.0 %all-gather.25.cloned.1.call-start = ((), (), s32[]{:S(2)}) async-start(), calls=%async_computation.8 | async-start | bytes 1114112 | tf_op jit(solution)/shard_map/all_gather | solution.py:25
  282.9 271.9 %all-gather.27.cloned.1.call-start = ((), (), s32[]{:S(2)}) async-start(), calls=%async_computation.9 | async-start | bytes 3342336 | tf_op jit(solution)/shard_map/all_gather | solution.py:24
  283.6 383.4 %all-reduce.9.cloned.1.call-start = ((), (), s32[]{:S(2)}) async-start(), calls=%async_computation.2 | async-start | bytes 3145728 | tf_op jit(solution)/shard_map/psum | solution.py:9
  447.0 12.9 %copy-start.2 = (f32[512,768]{0,1:T(8,128)S(1)}, f32[512,768]{0,1:T(8,128)}, u32[]{:S(2)}) copy-start(f32[512,768]{0,1:T(8,128)} %all-reduce.7.cloned.1.call-done) | copy-start | bytes 4718596
  501.6 218.3 %all-gather.29.cloned.1.call-start = ((), (), s32[]{:S(2)}) async-start(), calls=%async_computation.10 | async-start | bytes 1114112 | tf_op jit(solution)/shard_map/all_gather | solution.py:25
  502.4 272.2 %all-gather.31.cloned.1.call-start = ((), (), s32[]{:S(2)}) async-start(), calls=%async_computation.11 | async-start | bytes 3342336 | tf_op jit(solution)/shard_map/all_gather | solution.py:24
  503.1 383.6 %all-reduce.11.cloned.1.call-start = ((), (), s32[]{:S(2)}) async-start(), calls=%async_computation.3 | async-start | bytes 3145728 | tf_op jit(solution)/shard_map/psum | solution.py:9
  667.0 12.9 %copy-start.1 = (f32[512,768]{0,1:T(8,128)S(1)}, f32[512,768]{0,1:T(8,128)}, u32[]{:S(2)}) copy-start(f32[512,768]{0,1:T(8,128)} %all-reduce.9.cloned.1.call-done) | copy-start | bytes 4718596
  886.8 13.1 %copy-start.3 = (f32[512,768]{0,1:T(8,128)S(1)}, f32[512,768]{0,1:T(8,128)}, u32[]{:S(2)}) copy-start(f32[512,768]{0,1:T(8,128)} %all-reduce.11.cloned.1.call-done) | copy-start | bytes 4718596
Sparse Core Ops, SparseCore 0:
  9.8 50.0 all-gather.16
  62.9 110.4 all-reduce.4
  175.8 55.8 all-gather.18
  234.1 46.2 all-gather.20
  282.7 52.1 all-gather.22
  337.1 109.8 all-reduce.6
  449.5 50.5 all-gather.24
  502.5 52.1 all-gather.26
  557.1 109.8 all-reduce.8
  669.3 50.5 all-gather.28
  722.4 52.1 all-gather.30
  776.8 109.8 all-reduce.10
where the time goes:
time: 920 us; the launch traced here: 916 us
  waiting for transfers between devices  813 us (88%)
  matrix products  50.9 us (6%)
  local copies, waits for them, and re-layouts  19.8 us (2%)
  other arithmetic  17.1 us (2%)
  between operations  13.7 us (1%)
    psum x4, waiting for transfers between devices, spread(): return lax.psum(jnp.where(mine, x, jnp.zeros_like(x)), axis)  438 us
    all_gather x4, waiting for transfers between devices, per_device(): factor_cols = lax.all_gather(panels_l[k], 'col', axis=1, tiled=True)  214 us
    all_gather x4, waiting for transfers between devices, per_device(): inverse_tile = lax.all_gather(diag_inverse[k], 'col', axis=1, tiled=True)  160 us
    dot_general x4, matrix products, exact_dot(): jnp.dot(left, right, precision=lax.Precision.HIGHEST, preferred_element_t...  50.9 us
  transfers between devices with their start and end apart: 12, of which 12 were waited for; matrix products, arithmetic and copies ran while one was open for 7% of the time, Pallas kernels for 0%

commit v1 on v0

v1 whole, which is shorter than its diff:
```python
import functools

import jax
import jax.numpy as jnp
from jax import lax
from jax.experimental import pallas as pl
from jax.experimental.pallas import tpu as pltpu
from jax.sharding import PartitionSpec as P

MESH = pl.DeviceIdType.MESH
F32, BF16 = jnp.float32, jnp.bfloat16

UNITS = 12
PIECES = 8
SPOTS = 8
TURNS = 15
S_FIRST, S_HOP, S_NUM, S_DEN = 24, 4, 5, 8


def split(v):
    high = v.astype(BF16)
    return high, (v - high.astype(F32)).astype(BF16)


def kernel(
    rhs, pan, diag, out, share, solved, right3, left3,
    io_sem, take_sem, l_recv, l_send, c_recv, c_send, b_recv, b_send, x_send,
):
    row, col = lax.axis_index("row"), lax.axis_index("col")
    z, core = row // 2, row % 2
    y, x = col // 4, col % 4
    rows = out.shape[0]
    panel = solved.shape[1]
    slab = pan.shape[1]
    half_panel = panel // 2
    piece = half_panel // PIECES
    sibling = row + 1 - 2 * core
    down = (row + 2 - 4 * core + 16) % 16
    up = (row - 2 + 4 * core + 16) % 16
    hops = jnp.where(core == 0, z, (8 - z) % 8)

    def at_plane(dy, dx):
        return (row, ((y + dy + 8) % 4) * 4 + (x + dx + 8) % 4)

    def source(ry, rx):
        return ((y + ry + 8) % 4) * 4 + (x + rx + 8) % 4

    def relative(ry, rx):
        return ((ry + 8) % 4) * 4 + (rx + 8) % 4


    def tile_part(unit, part, ry, rx):
        size = slab if part is None else slab // 2
        start = source(ry, rx) * slab + (slab // 2 if part == 1 else 0)
        return share.at[unit, pl.ds(pl.multiple_of(start, slab // 2), size), :]

    def send(unit, part, src, to, slot):
        ref = tile_part(unit, part, *src)
        pltpu.make_async_remote_copy(
            src_ref=ref, dst_ref=ref,
            send_sem=l_send.at[unit, slot],
            recv_sem=l_recv.at[unit, part or 0, relative(src[0] - to[0], src[1] - to[1])],
            device_id=at_plane(*to), device_id_type=MESH,
        ).start()

    def arrive(unit, part, ry, rx):
        ref = tile_part(unit, part, ry, rx)
        pltpu.make_async_remote_copy(
            src_ref=ref, dst_ref=ref,
            send_sem=l_send.at[unit, 0],
            recv_sem=l_recv.at[unit, part or 0, relative(ry, rx)],
            device_id=at_plane(0, 1), device_id_type=MESH,
        ).wait_recv()

    def stage0(unit):
        for slot, to in enumerate(((0, 1), (0, -1), (1, 0), (-1, 0))):
            send(unit, None, (0, 0), to, slot)

    def stage1(unit, step):
        e = 1 - 2 * (unit % 2)
        if step == 0:
            arrive(unit, None, 0, -e)
            send(unit, 0, (0, -e), (0, e), 4)
            send(unit, 0, (0, -e), (1, 0), 5)
            send(unit, 0, (0, -e), (-1, 0), 6)
        elif step == 1:
            arrive(unit, None, e, 0)
            send(unit, 1, (e, 0), (-e, 0), 7)
            send(unit, 1, (e, 0), (0, 1), 8)
            send(unit, 1, (e, 0), (0, -1), 9)
        elif step == 2:
            arrive(unit, None, 0, e)
            send(unit, 0, (0, e), (1, 0), 10)
            send(unit, 0, (0, e), (-1, 0), 11)
            send(unit, 1, (0, e), (0, -e), 12)
        else:
            arrive(unit, None, -e, 0)
            send(unit, 1, (-e, 0), (0, 1), 13)
            send(unit, 1, (-e, 0), (0, -1), 14)
            send(unit, 0, (-e, 0), (e, 0), 15)

    def stage2(unit, step):
        e = 1 - 2 * (unit % 2)
        if step == 0:
            arrive(unit, 0, 0, 2)
            send(unit, 0, (0, 2), (1, 0), 16)
            send(unit, 0, (0, 2), (-1, 0), 17)
            arrive(unit, 1, 2, 0)
            send(unit, 1, (2, 0), (0, 1), 18)
            send(unit, 1, (2, 0), (0, -1), 19)
        elif step == 1:
            arrive(unit, 0, -e, 1)
            send(unit, 0, (-e, 1), (e, 0), 20)
            arrive(unit, 1, 1, e)
            send(unit, 1, (1, e), (0, -e), 21)
        else:
            arrive(unit, 0, -e, -1)
            send(unit, 0, (-e, -1), (e, 0), 22)
            arrive(unit, 1, -1, e)
            send(unit, 1, (-1, e), (0, -e), 23)

    def stage3(unit):
        e = 1 - 2 * (unit % 2)
        arrive(unit, 0, -e, 2)
        send(unit, 0, (-e, 2), (e, 0), 24)
        arrive(unit, 1, 2, e)
        send(unit, 1, (2, e), (0, -e), 25)

    def final(unit):
        e = 1 - 2 * (unit % 2)
        for ry, rx in ((e, 1), (e, -1), (2, 0), (e, 2), (2, 1), (2, -1), (2, 2)):
            arrive(unit, 0, ry, rx)
        for ry, rx in ((1, -e), (-1, -e), (0, 2), (2, -e), (1, 2), (-1, 2), (2, 2)):
            arrive(unit, 1, ry, rx)

    def drain_shares(count):
        def body(unit, _):
            for slot in range(26):
                ref = tile_part(unit, None if slot < 4 else 0, 0, 0)
                pltpu.make_async_remote_copy(
                    src_ref=ref, dst_ref=ref,
                    send_sem=l_send.at[unit, slot], recv_sem=l_recv.at[unit, 0, 0],
                    device_id=at_plane(0, 1), device_id_type=MESH,
                ).wait_send()
            return 0

        lax.fori_loop(0, count, body, 0)


    def strip(k, which, p):
        start = pl.multiple_of(which * half_panel + p * piece, piece)
        return solved.at[k, pl.ds(start, piece), :]

    def hop(k, which, p, send_sem, recv_sem, to):
        ref = strip(k, which, p)
        return pltpu.make_async_remote_copy(
            src_ref=ref, dst_ref=ref, send_sem=send_sem.at[k, p], recv_sem=recv_sem.at[k, p],
            device_id=(to, col), device_id_type=MESH,
        )

    def relay(j, to_sibling):
        k, p = j // PIECES, j % PIECES
        hop(k, core, p, c_send, c_recv, up).wait_recv()

        @pl.when(hops < 7)
        def _():
            hop(k, core, p, c_send, c_recv, down).start()

        if to_sibling:
            hop(k, core, p, b_send, b_recv, sibling).start()

    def from_sibling(k):
        for p in range(PIECES):
            hop(k, 1 - core, p, b_send, b_recv, sibling).wait_recv()


    def convert(src):
        def body(b, _):
            start = pl.multiple_of(b * 32, 32)
            high, low = split(src[pl.ds(start, 32), :])
            right3[pl.ds(start, 32), :] = high
            right3[pl.ds(pl.multiple_of(panel + start, 32), 32), :] = low
            right3[pl.ds(pl.multiple_of(2 * panel + start, 32), 32), :] = high
            return 0

        lax.fori_loop(0, panel // 32, body, 0)

    def unfold(unit):
        def body(b, _):
            start = pl.multiple_of(b * 128, 128)
            for g in range(panel // 128):
                tile = share[unit, pl.ds(start, 128), g * 128 : (g + 1) * 128].T
                high, low = split(tile)
                to = pl.ds(g * 128, 128)
                left3[to, pl.ds(start, 128)] = high
                left3[to, pl.ds(pl.multiple_of(panel + start, 128), 128)] = high
                left3[to, pl.ds(pl.multiple_of(2 * panel + start, 128), 128)] = low
            return 0

        lax.fori_loop(0, panel // 128, body, 0)

    def product(block, dest):
        cols = pl.ds(pl.multiple_of(block * 256, 256), 256)
        to = pl.ds(pl.multiple_of(dest * panel, panel), panel)
        acc = jnp.dot(left3[...], right3[:, cols], preferred_element_type=F32)
        return cols, to, acc

    def subtract(block, dest):
        cols, to, acc = product(block, dest)
        out[to, cols] = out[to, cols] - acc

    def assign(block, dest, k):
        cols, to, acc = product(block, dest)
        out[to, cols] = acc
        solved[k, :, cols] = acc

    def subtract_all(dest):
        def body(block, _):
            subtract(block, dest)
            return 0

        lax.fori_loop(0, 3, body, 0)

    def assign_all(dest, k):
        def body(block, _):
            assign(block, dest, k)
            return 0

        lax.fori_loop(0, 3, body, 0)

    def out_panel(u):
        return out.at[pl.ds(pl.multiple_of(u * panel, panel), panel), :]


    first, second = row == 0, row == 1

    def loop(first, last, body):
        def turn(i, _):
            body(i)
            return 0

        lax.fori_loop(first, last, turn, 0)

    fetch = pltpu.make_async_copy(rhs, out, io_sem.at[0])
    fetch.start()

    def mine(t):
        return share.at[t, pl.ds(pl.multiple_of(col * slab, slab), slab), :]

    def take_factor(t, k, u):
        columns = pl.ds(pl.multiple_of(u * panel, panel), panel)
        return pltpu.make_async_copy(pan.at[k, :, columns], mine(t), take_sem.at[t])

    def take_inverse(t, k):
        return pltpu.make_async_copy(diag.at[k], mine(t), take_sem.at[t])

    @pl.when(row > 1)
    def _():
        loop(0, UNITS, lambda t: take_factor(t, t // 3, t % 3).start())

    @pl.when(first)
    def _():
        take_inverse(0, 0).start()
        take_factor(1, 0, 1).start()
        take_factor(2, 0, 2).start()
        take_inverse(3, 1).start()
        take_factor(4, 1, 2).start()
        take_inverse(5, 2).start()

    @pl.when(second)
    def _():
        loop(0, 3, lambda t: take_factor(t, t, 0).start())
        take_inverse(3, 3).start()
        loop(4, UNITS, lambda t: take_factor(t, (t - 4) // 2, 1 + t % 2).start())

    barrier = pltpu.get_barrier_semaphore()
    for to in (at_plane(0, 1), at_plane(0, -1), at_plane(1, 0), at_plane(-1, 0), (sibling, col), (up, col), (down, col)):
        pl.semaphore_signal(barrier, inc=1, device_id=to, device_id_type=MESH)

    loop(0, jnp.where(first, 6, UNITS), lambda t: take_inverse(t, 0).wait())
    pl.semaphore_wait(barrier, 7)
    fetch.wait()


    def plane_turn(m, count):
        @pl.when(m + 2 < count)
        def _():
            stage0(m + 2)

        @pl.when(m < count)
        def _():
            for i in range(4):
                stage1(m, i)

        @pl.when(m >= 1)
        def _():
            for i in range(3):
                stage2(m - 1, i)
            stage3(m - 1)

    @pl.when(first)
    def _():
        stage0(0)
        stage0(1)

        def turn(m):
            plane_turn(m, 6)

            @pl.when(m >= 1)
            def _():
                q = m - 1
                final(q)
                k = jnp.where(q < 3, 0, jnp.where(q < 5, 1, 2))
                dest = jnp.where(q < 3, q, jnp.where(q < 4, 1, 2))
                is_solve = (q == 0) | (q == 3) | (q == 5)

                @pl.when(q != 2)
                def _():
                    convert(out_panel(k))

                unfold(q)

                @pl.when(is_solve)
                def _():
                    assign_all(dest, k)
                    for p in range(PIECES):
                        hop(k, 0, p, c_send, c_recv, down).start()
                        hop(k, 1, p, x_send, c_recv, sibling).start()
                        hop(k, 0, p, b_send, b_recv, sibling).start()

                @pl.when(jnp.logical_not(is_solve))
                def _():
                    subtract_all(dest)

        loop(0, 7, turn)
        loop(3 * PIECES, 4 * PIECES, lambda j: relay(j, False))
        drain_shares(6)

        def drain(j):
            k, p = j // PIECES, j % PIECES
            hop(k, 0, p, c_send, c_recv, down).wait_send()

            @pl.when(k < 3)
            def _():
                hop(k, 1, p, x_send, c_recv, sibling).wait_send()
                hop(k, 0, p, b_send, b_recv, sibling).wait_send()

        loop(0, 4 * PIECES, drain)

    @pl.when(second)
    def _():
        loop(0, PIECES, lambda j: relay(j, False))
        from_sibling(0)
        stage0(0)
        stage0(1)

        def turn(m):
            plane_turn(m, UNITS)

            @pl.when(m >= 1)
            def _():
                q = m - 1
                final(q)

                @pl.when((q == 1) | (q == 2))
                def _():
                    loop(q * PIECES, (q + 1) * PIECES, lambda j: relay(j, False))
                    from_sibling(q)

                @pl.when(q == 3)
                def _():
                    convert(out_panel(0))

                @pl.when((q < 3) | ((q >= 4) & (q % 2 == 0)))
                def _():
                    convert(solved.at[jnp.where(q < 3, q, (q - 4) // 2)])

                unfold(q)

                @pl.when(q == 3)
                def _():
                    assign_all(0, 3)
                    for p in range(PIECES):
                        hop(3, 1, p, c_send, c_recv, down).start()
                        hop(3, 0, p, x_send, c_recv, sibling).start()

                @pl.when(q != 3)
                def _():
                    subtract_all(jnp.where(q < 3, 0, 1 + q % 2))

        loop(0, UNITS + 1, turn)
        drain_shares(UNITS)
        loop(0, 4 * PIECES, lambda j: hop(j // PIECES, 1, j % PIECES, c_send, c_recv, down).wait_send())
        loop(0, PIECES, lambda p: hop(3, 0, p, x_send, c_recv, sibling).wait_send())


    @pl.when(row > 1)
    def _():
        farthest = jnp.maximum(hops, 8 - hops)
        lag = (S_FIRST + S_HOP * farthest + 16 + 3) // 4

        def relayed(spot):
            ahead = jnp.maximum(spot - S_FIRST - S_HOP * hops, 0)
            return jnp.minimum(ahead * S_NUM // S_DEN, 4 * PIECES)

        def taken(slot):
            ready = jnp.minimum(slot - lag, jnp.maximum(slot - 4, 0) // 2 - 1)
            return jnp.clip(ready + 1, 0, UNITS)

        stage0(0)
        stage0(1)

        def turn(m):
            for i in range(SPOTS):
                if i == 0:

                    @pl.when(m + 2 < UNITS)
                    def _():
                        stage0(m + 2)

                if i < 4:

                    @pl.when(m < UNITS)
                    def _():
                        stage1(m, i)
                elif i < 7:

                    @pl.when((m >= 1) & (m < UNITS + 1))
                    def _():
                        stage2(m - 1, i - 4)
                else:

                    @pl.when((m >= 2) & (m < UNITS + 2))
                    def _():
                        stage3(m - 2)

                spot = m * SPOTS + i
                loop(relayed(spot - 1), relayed(spot), lambda j: relay(j, True))

                slot = 2 * m + i // 4
                q = taken(slot) - 1
                fresh = q >= taken(slot - 1)
                part = i % 4
                if part == 0:

                    @pl.when(fresh)
                    def _():
                        final(q)

                        @pl.when(q % 3 == 0)
                        def _():
                            from_sibling(q // 3)
                            convert(solved.at[q // 3])

                        unfold(q)
                else:

                    @pl.when(fresh)
                    def _():
                        subtract(part - 1, q % 3)

        loop(0, TURNS, turn)
        drain_shares(UNITS)

        def drain(j):
            k, p = j // PIECES, j % PIECES

            @pl.when(hops < 7)
            def _():
                hop(k, core, p, c_send, c_recv, down).wait_send()

            hop(k, core, p, b_send, b_recv, sibling).wait_send()

        loop(0, 4 * PIECES, drain)


def per_device(rhs, panels_l, diag_inverse):
    rows, width = rhs.shape
    count, panel, _ = diag_inverse.shape
    sem = pltpu.SemaphoreType.DMA
    return pl.pallas_call(
        kernel,
        out_shape=jax.ShapeDtypeStruct((rows, width), F32),
        in_specs=[pl.BlockSpec(memory_space=pl.ANY)] * 3,
        out_specs=pl.BlockSpec(memory_space=pltpu.VMEM),
        scratch_shapes=[
            pltpu.VMEM((UNITS, panel, panel), F32),
            pltpu.VMEM((count, panel, width), F32),
            pltpu.VMEM((3 * panel, width), BF16),
            pltpu.VMEM((panel, 3 * panel), BF16),
            sem((1,)),
            sem((UNITS,)),
            sem((UNITS, 2, 16)),
            sem((UNITS, 26)),
            sem((count, PIECES)),
            sem((count, PIECES)),
            sem((count, PIECES)),
            sem((count, PIECES)),
            sem((count, PIECES)),
        ],
        compiler_params=pltpu.CompilerParams(
            collective_id=0, has_side_effects=True, vmem_limit_bytes=60 * 1024 * 1024
        ),
        name="forward_substitution",
    )(rhs, jnp.swapaxes(panels_l, 1, 2), jnp.swapaxes(diag_inverse, 1, 2))


def solution(mesh):
    in_specs = (P("row", "col"), P(None, "row", "col"), P(None, None, "col"))
    out_specs = P("row", "col")
    return jax.shard_map(
        per_device, mesh=mesh, in_specs=in_specs, out_specs=out_specs, check_vma=False
    )
```

time: 920 us -> 181 us (0.20)
  the two profiles are of different devices: /device:TPU:32 before, /device:TPU:1 now
where the time goes in v1:
time: 181 us
  Pallas kernels  176 us (97%)
  local copies, waits for them, and re-layouts  4.83 us (3%)
    pallas_call x1, Pallas kernels, per_device(): pl.pallas_call(kernel, out_shape=jax.ShapeDtypeStruct((rows, width), F32)...  176 us
    unnamed x1, local copies, waits for them, and re-layouts  4.83 us

profile of v1, /device:TPU:1, one launch (start us, length us, event | category | flops | bytes accessed | tf_op | source)
XLA Modules:
  0.0 181.2 jit_solution(9811759790153260848)
XLA Ops:
  0.0 176.3 %forward_substitution.1 = f32[1536,768]{1,0:T(8,128)} custom-call(f32[1536,768]{1,0:T(8,128)} %rhs.1, f32[4,32,1536]{2,1,0:T(8,128)} %bitcast.2, f32[4,32,512]{2,1,0:T(8,128)} %bitcast.3), custom_call_target="tpu_custom_call" | custom-call | tf_op jit(solution)/shard_map/forward_substitution/pallas_call | solution.py:481
  176.3 4.8 %copy.5 = f32[1536,768]{1,0:T(8,128)} copy(f32[1536,768]{1,0:T(8,128)} %forward_substitution.1) | data formatting | bytes 9437184

commit v2 on v1

--- a/solution.py
+++ b/solution.py
@@ -11,10 +11,14 @@
 F32, BF16 = jnp.float32, jnp.bfloat16
 
 UNITS = 12
-PIECES = 8
+PIECES = 16
+GROUP = 4
 SPOTS = 8
-TURNS = 15
-S_FIRST, S_HOP, S_NUM, S_DEN = 24, 4, 5, 8
+S_FIRST, S_HOP, S_NUM, S_DEN = 24, 4, 5, 4
+GO = 3
+LAG = -(-(S_FIRST + 7 * S_HOP + 16) // 4)
+SLACK = 11
+TURNS = -(-max(UNITS + LAG, 2 * UNITS - 1 + SLACK) // 4)
 
 
 def split(v):
@@ -24,7 +28,7 @@
 
 def kernel(
     rhs, pan, diag, out, share, solved, right3, left3,
-    io_sem, take_sem, l_recv, l_send, c_recv, c_send, b_recv, b_send, x_send,
+    go_sem, io_sem, take_sem, l_recv, l_send, c_recv, c_send, b_recv, b_send, x_send,
 ):
     row, col = lax.axis_index("row"), lax.axis_index("col")
     z, core = row // 2, row % 2
@@ -32,27 +36,29 @@
     rows = out.shape[0]
     panel = solved.shape[1]
     slab = pan.shape[1]
-    half_panel = panel // 2
+    half_slab, half_panel = slab // 2, panel // 2
     piece = half_panel // PIECES
     sibling = row + 1 - 2 * core
     down = (row + 2 - 4 * core + 16) % 16
     up = (row - 2 + 4 * core + 16) % 16
     hops = jnp.where(core == 0, z, (8 - z) % 8)
 
+    ys = [lax.rem(y + d, 4) for d in range(4)]
+    xs = [lax.rem(x + d, 4) for d in range(4)]
+    sources = [[4 * ys[ry] + xs[rx] for rx in range(4)] for ry in range(4)]
+    starts = [[slab * v for v in line] for line in sources]
+
     def at_plane(dy, dx):
-        return (row, ((y + dy + 8) % 4) * 4 + (x + dx + 8) % 4)
-
-    def source(ry, rx):
-        return ((y + ry + 8) % 4) * 4 + (x + rx + 8) % 4
+        return (row, sources[dy % 4][dx % 4])
 
     def relative(ry, rx):
-        return ((ry + 8) % 4) * 4 + (rx + 8) % 4
+        return (ry % 4) * 4 + rx % 4
 
 
     def tile_part(unit, part, ry, rx):
-        size = slab if part is None else slab // 2
-        start = source(ry, rx) * slab + (slab // 2 if part == 1 else 0)
-        return share.at[unit, pl.ds(pl.multiple_of(start, slab // 2), size), :]
+        start = starts[ry % 4][rx % 4] + (half_slab if part == 1 else 0)
+        size = slab if part is None else half_slab
+        return share.at[unit, pl.ds(pl.multiple_of(start, half_slab), size), :]
 
     def send(unit, part, src, to, slot):
         ref = tile_part(unit, part, *src)
@@ -76,8 +82,7 @@
         for slot, to in enumerate(((0, 1), (0, -1), (1, 0), (-1, 0))):
             send(unit, None, (0, 0), to, slot)
 
-    def stage1(unit, step):
-        e = 1 - 2 * (unit % 2)
+    def stage1(unit, e, step):
         if step == 0:
             arrive(unit, None, 0, -e)
             send(unit, 0, (0, -e), (0, e), 4)
@@ -99,8 +104,7 @@
             send(unit, 1, (-e, 0), (0, -1), 14)
             send(unit, 0, (-e, 0), (e, 0), 15)
 
-    def stage2(unit, step):
-        e = 1 - 2 * (unit % 2)
+    def stage2(unit, e, step):
         if step == 0:
             arrive(unit, 0, 0, 2)
             send(unit, 0, (0, 2), (1, 0), 16)
@@ -119,19 +123,22 @@
             arrive(unit, 1, -1, e)
             send(unit, 1, (-1, e), (0, -e), 23)
 
-    def stage3(unit):
-        e = 1 - 2 * (unit % 2)
+    def stage3(unit, e):
         arrive(unit, 0, -e, 2)
         send(unit, 0, (-e, 2), (e, 0), 24)
         arrive(unit, 1, 2, e)
         send(unit, 1, (2, e), (0, -e), 25)
 
     def final(unit):
-        e = 1 - 2 * (unit % 2)
-        for ry, rx in ((e, 1), (e, -1), (2, 0), (e, 2), (2, 1), (2, -1), (2, 2)):
-            arrive(unit, 0, ry, rx)
-        for ry, rx in ((1, -e), (-1, -e), (0, 2), (2, -e), (1, 2), (-1, 2), (2, 2)):
-            arrive(unit, 1, ry, rx)
+        def rest(e):
+            for ry, rx in ((e, 1), (e, -1), (2, 0), (e, 2), (2, 1), (2, -1), (2, 2)):
+                arrive(unit, 0, ry, rx)
+            for ry, rx in ((1, -e), (-1, -e), (0, 2), (2, -e), (1, 2), (-1, 2), (2, 2)):
+                arrive(unit, 1, ry, rx)
+
+        even = lax.rem(unit, 2) == 0
+        pl.when(even)(lambda: rest(1))
+        pl.when(jnp.logical_not(even))(lambda: rest(-1))
 
     def drain_shares(count):
         def body(unit, _):
@@ -159,7 +166,7 @@
         )
 
     def relay(j, to_sibling):
-        k, p = j // PIECES, j % PIECES
+        k, p = lax.div(j, PIECES), lax.rem(j, PIECES)
         hop(k, core, p, c_send, c_recv, up).wait_recv()
 
         @pl.when(hops < 7)
@@ -167,11 +174,22 @@
             hop(k, core, p, c_send, c_recv, down).start()
 
         if to_sibling:
-            hop(k, core, p, b_send, b_recv, sibling).start()
+
+            @pl.when(lax.rem(p, GROUP) == GROUP - 1)
+            def _():
+                beside(k, core, lax.div(p, GROUP)).start()
+
+    def beside(k, which, g):
+        rows = GROUP * piece
+        ref = solved.at[k, pl.ds(pl.multiple_of(which * half_panel + g * rows, rows), rows), :]
+        return pltpu.make_async_remote_copy(
+            src_ref=ref, dst_ref=ref, send_sem=b_send.at[k, g], recv_sem=b_recv.at[k, g],
+            device_id=(sibling, col), device_id_type=MESH,
+        )
 
     def from_sibling(k):
-        for p in range(PIECES):
-            hop(k, 1 - core, p, b_send, b_recv, sibling).wait_recv()
+        for g in range(PIECES // GROUP):
+            beside(k, 1 - core, g).wait_recv()
 
 
     def convert(src):
@@ -279,24 +297,31 @@
 
     loop(0, jnp.where(first, 6, UNITS), lambda t: take_inverse(t, 0).wait())
     pl.semaphore_wait(barrier, 7)
-    fetch.wait()
-
-
-    def plane_turn(m, count):
-        @pl.when(m + 2 < count)
+
+
+    def plane_turn(m, first_unit, last_unit):
+        @pl.when(m + 2 < last_unit)
         def _():
             stage0(m + 2)
 
-        @pl.when(m < count)
-        def _():
-            for i in range(4):
-                stage1(m, i)
-
-        @pl.when(m >= 1)
-        def _():
-            for i in range(3):
-                stage2(m - 1, i)
-            stage3(m - 1)
+        def relays(e):
+            @pl.when(m < last_unit)
+            def _():
+                for i in range(4):
+                    stage1(m, e, i)
+
+            @pl.when((m >= first_unit + 1) & (m < last_unit + 1))
+            def _():
+                for i in range(3):
+                    stage2(m - 1, -e, i)
+
+            @pl.when((m >= first_unit + 2) & (m < last_unit + 2))
+            def _():
+                stage3(m - 2, e)
+
+        even = lax.rem(m, 2) == 0
+        pl.when(even)(lambda: relays(1))
+        pl.when(jnp.logical_not(even))(lambda: relays(-1))
 
     @pl.when(first)
     def _():
@@ -304,11 +329,19 @@
         stage0(1)
 
         def turn(m):
-            plane_turn(m, 6)
-
-            @pl.when(m >= 1)
-            def _():
-                q = m - 1
+            @pl.when(m == GO)
+            def _():
+                pl.semaphore_signal(go_sem, inc=1, device_id=(sibling, col), device_id_type=MESH)
+
+            plane_turn(m, 0, 6)
+
+            @pl.when(m == 3)
+            def _():
+                fetch.wait()
+
+            @pl.when(m >= 3)
+            def _():
+                q = m - 3
                 final(q)
                 k = jnp.where(q < 3, 0, jnp.where(q < 5, 1, 2))
                 dest = jnp.where(q < 3, q, jnp.where(q < 4, 1, 2))
@@ -326,13 +359,14 @@
                     for p in range(PIECES):
                         hop(k, 0, p, c_send, c_recv, down).start()
                         hop(k, 1, p, x_send, c_recv, sibling).start()
-                        hop(k, 0, p, b_send, b_recv, sibling).start()
+                    for g in range(PIECES // GROUP):
+                        beside(k, 0, g).start()
 
                 @pl.when(jnp.logical_not(is_solve))
                 def _():
                     subtract_all(dest)
 
-        loop(0, 7, turn)
+        loop(0, 9, turn)
         loop(3 * PIECES, 4 * PIECES, lambda j: relay(j, False))
         drain_shares(6)
 
@@ -343,37 +377,40 @@
             @pl.when(k < 3)
             def _():
                 hop(k, 1, p, x_send, c_recv, sibling).wait_send()
-                hop(k, 0, p, b_send, b_recv, sibling).wait_send()
+
+                @pl.when(lax.rem(p, GROUP) == 0)
+                def _():
+                    beside(k, 0, lax.div(p, GROUP)).wait_send()
 
         loop(0, 4 * PIECES, drain)
 
     @pl.when(second)
     def _():
-        loop(0, PIECES, lambda j: relay(j, False))
-        from_sibling(0)
+        pl.semaphore_wait(go_sem, 1)
         stage0(0)
         stage0(1)
 
-        def turn(m):
-            plane_turn(m, UNITS)
-
-            @pl.when(m >= 1)
-            def _():
-                q = m - 1
+        def early_turn(m):
+            plane_turn(m, 0, 4)
+
+            @pl.when(m == 3)
+            def _():
+                fetch.wait()
+
+            @pl.when(m >= 3)
+            def _():
+                q = m - 3
                 final(q)
 
-                @pl.when((q == 1) | (q == 2))
+                @pl.when(q < 3)
                 def _():
                     loop(q * PIECES, (q + 1) * PIECES, lambda j: relay(j, False))
                     from_sibling(q)
+                    convert(solved.at[q])
 
                 @pl.when(q == 3)
                 def _():
                     convert(out_panel(0))
-
-                @pl.when((q < 3) | ((q >= 4) & (q % 2 == 0)))
-                def _():
-                    convert(solved.at[jnp.where(q < 3, q, (q - 4) // 2)])
 
                 unfold(q)
 
@@ -386,9 +423,28 @@
 
                 @pl.when(q != 3)
                 def _():
-                    subtract_all(jnp.where(q < 3, 0, 1 + q % 2))
-
-        loop(0, UNITS + 1, turn)
+                    subtract_all(0)
+
+        loop(0, 7, early_turn)
+        stage0(4)
+        stage0(5)
+
+        def turn(m):
+            plane_turn(m, 4, UNITS)
+
+            @pl.when(m >= 7)
+            def _():
+                q = m - 3
+                final(q)
+
+                @pl.when(q % 2 == 0)
+                def _():
+                    convert(solved.at[(q - 4) // 2])
+
+                unfold(q)
+                subtract_all(1 + q % 2)
+
+        loop(4, UNITS + 3, turn)
         drain_shares(UNITS)
         loop(0, 4 * PIECES, lambda j: hop(j // PIECES, 1, j % PIECES, c_send, c_recv, down).wait_send())
         loop(0, PIECES, lambda p: hop(3, 0, p, x_send, c_recv, sibling).wait_send())
@@ -397,20 +453,22 @@
     @pl.when(row > 1)
     def _():
         farthest = jnp.maximum(hops, 8 - hops)
-        lag = (S_FIRST + S_HOP * farthest + 16 + 3) // 4
+        lag = lax.div(S_FIRST + S_HOP * farthest + 16 + 3, 4)
+        due = S_FIRST + S_HOP * hops
 
         def relayed(spot):
-            ahead = jnp.maximum(spot - S_FIRST - S_HOP * hops, 0)
-            return jnp.minimum(ahead * S_NUM // S_DEN, 4 * PIECES)
+            ahead = jnp.maximum(spot - due, 0)
+            return jnp.minimum(lax.div(ahead * S_NUM, S_DEN), 4 * PIECES)
 
         def taken(slot):
-            ready = jnp.minimum(slot - lag, jnp.maximum(slot - 4, 0) // 2 - 1)
-            return jnp.clip(ready + 1, 0, UNITS)
+            ready = jnp.minimum(slot - lag + 1, lax.div(jnp.maximum(slot - SLACK + 2, 0), 2))
+            return jnp.clip(ready, 0, UNITS)
 
         stage0(0)
         stage0(1)
 
-        def turn(m):
+        def tile_turn(m, e, carry):
+            before, done = carry
             for i in range(SPOTS):
                 if i == 0:
 
@@ -418,48 +476,61 @@
                     def _():
                         stage0(m + 2)
 
-                if i < 4:
+                if i % 2 == 0:
 
                     @pl.when(m < UNITS)
                     def _():
-                        stage1(m, i)
+                        stage1(m, e, i // 2)
                 elif i < 7:
-
-                    @pl.when((m >= 1) & (m < UNITS + 1))
-                    def _():
-                        stage2(m - 1, i - 4)
-                else:
 
                     @pl.when((m >= 2) & (m < UNITS + 2))
                     def _():
-                        stage3(m - 2)
-
-                spot = m * SPOTS + i
-                loop(relayed(spot - 1), relayed(spot), lambda j: relay(j, True))
-
-                slot = 2 * m + i // 4
-                q = taken(slot) - 1
-                fresh = q >= taken(slot - 1)
+                        stage2(m - 2, e, i // 2)
+                else:
+
+                    @pl.when((m >= 3) & (m < UNITS + 3))
+                    def _():
+                        stage3(m - 3, -e)
+
+                now = relayed(m * SPOTS + i)
+                loop(done, now, lambda j: relay(j, True))
+                done = now
+
                 part = i % 4
                 if part == 0:
+                    after = taken(2 * m + i // 4)
+                    q = after - 1
+                    k, u = lax.div(jnp.maximum(q, 0), 3), lax.rem(jnp.maximum(q, 0), 3)
+                    fresh = after > before
+                    before = after
 
                     @pl.when(fresh)
                     def _():
                         final(q)
 
-                        @pl.when(q % 3 == 0)
+                        @pl.when(q == 0)
                         def _():
-                            from_sibling(q // 3)
-                            convert(solved.at[q // 3])
+                            fetch.wait()
+
+                        @pl.when(u == 0)
+                        def _():
+                            from_sibling(k)
+                            convert(solved.at[k])
 
                         unfold(q)
                 else:
 
                     @pl.when(fresh)
                     def _():
-                        subtract(part - 1, q % 3)
-
-        loop(0, TURNS, turn)
+                        subtract(part - 1, u)
+
+            return before, done
+
+        def turn(t, carry):
+            carry = tile_turn(2 * t, 1, carry)
+            return tile_turn(2 * t + 1, -1, carry)
+
+        lax.fori_loop(0, TURNS, turn, (jnp.int32(0), jnp.int32(0)))
         drain_shares(UNITS)
 
         def drain(j):
@@ -469,7 +540,9 @@
             def _():
                 hop(k, core, p, c_send, c_recv, down).wait_send()
 
-            hop(k, core, p, b_send, b_recv, sibling).wait_send()
+            @pl.when(lax.rem(p, GROUP) == 0)
+            def _():
+                beside(k, core, lax.div(p, GROUP)).wait_send()
 
         loop(0, 4 * PIECES, drain)
 
@@ -480,7 +553,7 @@
     sem = pltpu.SemaphoreType.DMA
     return pl.pallas_call(
         kernel,
-        out_shape=jax.ShapeDtypeStruct((rows, width), F32),
+        out_shape=pltpu.VMEM((rows, width), F32),
         in_specs=[pl.BlockSpec(memory_space=pl.ANY)] * 3,
         out_specs=pl.BlockSpec(memory_space=pltpu.VMEM),
         scratch_shapes=[
@@ -488,18 +561,19 @@
             pltpu.VMEM((count, panel, width), F32),
             pltpu.VMEM((3 * panel, width), BF16),
             pltpu.VMEM((panel, 3 * panel), BF16),
+            pltpu.SemaphoreType.REGULAR,
             sem((1,)),
             sem((UNITS,)),
             sem((UNITS, 2, 16)),
             sem((UNITS, 26)),
             sem((count, PIECES)),
             sem((count, PIECES)),
-            sem((count, PIECES)),
-            sem((count, PIECES)),
+            sem((count, PIECES // GROUP)),
+            sem((count, PIECES // GROUP)),
             sem((count, PIECES)),
         ],
         compiler_params=pltpu.CompilerParams(
-            collective_id=0, has_side_effects=True, vmem_limit_bytes=60 * 1024 * 1024
+            collective_id=0, has_side_effects=True, vmem_limit_bytes=62_200_000
         ),
         name="forward_substitution",
     )(rhs, jnp.swapaxes(panels_l, 1, 2), jnp.swapaxes(diag_inverse, 1, 2))

time: 181 us -> 115 us (0.64)
  the two profiles are of different devices: /device:TPU:1 before, /device:TPU:32 now
where the time goes in v2:
time: 115 us; the launch traced here: 113 us
  Pallas kernels  111 us (97%)
  local copies, waits for them, and re-layouts  2.19 us (2%)
    pallas_call x1, Pallas kernels, per_device(): pl.pallas_call(kernel, out_shape=pltpu.VMEM((rows, width), F32), in_specs...  111 us

profile of v2, /device:TPU:32, one launch (start us, length us, event | category | flops | bytes accessed | tf_op | source)
XLA Modules:
  0.0 113.3 jit_solution(965163331420470569)
XLA Ops:
  0.0 111.1 %forward_substitution.1 = f32[1536,768]{1,0:T(8,128)S(1)} custom-call(f32[1536,768]{1,0:T(8,128)} %rhs.1, f32[4,32,1536]{2,1,0:T(8,128)} %bitcast.2, f32[4,32,512]{2,1,0:T(8,128)} %bitcast.3), custom_call_target="tpu_custom_call" | custom-call | tf_op jit(solution)/shard_map/forward_substitution/pallas_call | solution.py:554
  111.2 2.2 %copy.5 = f32[1536,768]{1,0:T(8,128)} copy(f32[1536,768]{1,0:T(8,128)S(1)} %forward_substitution.1) | data formatting | bytes 9437184

commit v3 on v2

--- a/solution.py
+++ b/solution.py
@@ -11,11 +11,13 @@
 F32, BF16 = jnp.float32, jnp.bfloat16
 
 UNITS = 12
+HEAD, EARLY = 3, 7
+SLOTS = EARLY + 8
 PIECES = 16
 GROUP = 4
 SPOTS = 8
-S_FIRST, S_HOP, S_NUM, S_DEN = 24, 4, 5, 4
-GO = 3
+S_FIRST, S_HOP, S_NUM, S_DEN = 32, 4, 5, 4
+GO = 1
 LAG = -(-(S_FIRST + 7 * S_HOP + 16) // 4)
 SLACK = 11
 TURNS = -(-max(UNITS + LAG, 2 * UNITS - 1 + SLACK) // 4)
@@ -28,7 +30,7 @@
 
 def kernel(
     rhs, pan, diag, out, share, solved, right3, left3,
-    go_sem, io_sem, take_sem, l_recv, l_send, c_recv, c_send, b_recv, b_send, x_send,
+    go_sem, io_sem, take_sem, l_recv, l_send, c_recv, c_send, b_recv, b_send, x_send, h_recv, h_send,
 ):
     row, col = lax.axis_index("row"), lax.axis_index("col")
     z, core = row // 2, row % 2
@@ -232,6 +234,22 @@
         out[to, cols] = acc
         solved[k, :, cols] = acc
 
+    def subtract_ahead(k):
+        def body(block, _):
+            cols, _, acc = product(block, 0)
+            solved[k, :, cols] = solved[k, :, cols] - acc
+            return 0
+
+        lax.fori_loop(0, 3, body, 0)
+
+    def assign_ahead(k):
+        def body(block, _):
+            cols, _, acc = product(block, 0)
+            solved[k, :, cols] = acc
+            return 0
+
+        lax.fori_loop(0, 3, body, 0)
+
     def subtract_all(dest):
         def body(block, _):
             subtract(block, dest)
@@ -280,23 +298,47 @@
     def _():
         take_inverse(0, 0).start()
         take_factor(1, 0, 1).start()
-        take_factor(2, 0, 2).start()
-        take_inverse(3, 1).start()
-        take_factor(4, 1, 2).start()
-        take_inverse(5, 2).start()
+        take_inverse(2, 1).start()
 
     @pl.when(second)
     def _():
-        loop(0, 3, lambda t: take_factor(t, t, 0).start())
-        take_inverse(3, 3).start()
-        loop(4, UNITS, lambda t: take_factor(t, (t - 4) // 2, 1 + t % 2).start())
+        take_factor(0, 0, 0).start()
+        take_inverse(3, 2).start()
+        take_factor(4, 1, 0).start()
+        take_factor(5, 2, 0).start()
+        take_inverse(6, 3).start()
+        loop(0, 8, lambda j: take_factor(EARLY + j, lax.div(j, 2), 1 + lax.rem(j, 2)).start())
+
+    def handed(i):
+        columns = pl.ds(2 * panel, panel)
+        src, dst = (
+            (rhs.at[columns, :], solved.at[2]),
+            (pan.at[0, :, columns], mine(1)),
+            (pan.at[1, :, columns], mine(2)),
+            (solved.at[2], solved.at[2]),
+        )[i]
+        return pltpu.make_async_remote_copy(
+            src_ref=src, dst_ref=dst, send_sem=h_send.at[i], recv_sem=h_recv.at[i],
+            device_id=(sibling, col), device_id_type=MESH,
+        )
 
     barrier = pltpu.get_barrier_semaphore()
     for to in (at_plane(0, 1), at_plane(0, -1), at_plane(1, 0), at_plane(-1, 0), (sibling, col), (up, col), (down, col)):
         pl.semaphore_signal(barrier, inc=1, device_id=to, device_id_type=MESH)
 
-    loop(0, jnp.where(first, 6, UNITS), lambda t: take_inverse(t, 0).wait())
-    pl.semaphore_wait(barrier, 7)
+    for pair in ((1, 2), (2, 1)):
+
+        @pl.when(row == pair[0])
+        def _():
+            pl.semaphore_signal(barrier, inc=1, device_id=(pair[1], col), device_id_type=MESH)
+
+    loop(0, jnp.where(first, HEAD, jnp.where(second, 1, UNITS)), lambda t: take_inverse(t, 0).wait())
+
+    @pl.when(second)
+    def _():
+        loop(3, SLOTS, lambda t: take_inverse(t, 0).wait())
+
+    pl.semaphore_wait(barrier, jnp.where((row == 1) | (row == 2), 8, 7))
 
 
     def plane_turn(m, first_unit, last_unit):
@@ -325,15 +367,18 @@
 
     @pl.when(first)
     def _():
+        for i in (1, 2):
+            handed(i).start()
         stage0(0)
         stage0(1)
+        handed(0).start()
 
         def turn(m):
             @pl.when(m == GO)
             def _():
                 pl.semaphore_signal(go_sem, inc=1, device_id=(sibling, col), device_id_type=MESH)
 
-            plane_turn(m, 0, 6)
+            plane_turn(m, 0, HEAD)
 
             @pl.when(m == 3)
             def _():
@@ -343,111 +388,129 @@
             def _():
                 q = m - 3
                 final(q)
-                k = jnp.where(q < 3, 0, jnp.where(q < 5, 1, 2))
-                dest = jnp.where(q < 3, q, jnp.where(q < 4, 1, 2))
-                is_solve = (q == 0) | (q == 3) | (q == 5)
-
-                @pl.when(q != 2)
-                def _():
-                    convert(out_panel(k))
-
+                k = jnp.where(q < 2, 0, 1)
+                convert(out_panel(k))
                 unfold(q)
 
-                @pl.when(is_solve)
-                def _():
-                    assign_all(dest, k)
+                @pl.when(q != 1)
+                def _():
+                    assign_all(k, k)
                     for p in range(PIECES):
                         hop(k, 0, p, c_send, c_recv, down).start()
                         hop(k, 1, p, x_send, c_recv, sibling).start()
                     for g in range(PIECES // GROUP):
                         beside(k, 0, g).start()
 
-                @pl.when(jnp.logical_not(is_solve))
-                def _():
-                    subtract_all(dest)
-
-        loop(0, 9, turn)
-        loop(3 * PIECES, 4 * PIECES, lambda j: relay(j, False))
-        drain_shares(6)
+                @pl.when(q == 1)
+                def _():
+                    subtract_all(1)
+
+        loop(0, HEAD + 3, turn)
+        handed(3).wait_recv()
+        back = pltpu.make_async_copy(solved.at[2], out.at[pl.ds(2 * panel, panel), :], io_sem.at[0])
+        back.start()
+        drain_shares(HEAD)
 
         def drain(j):
-            k, p = j // PIECES, j % PIECES
+            k, p = lax.div(j, PIECES), lax.rem(j, PIECES)
             hop(k, 0, p, c_send, c_recv, down).wait_send()
-
-            @pl.when(k < 3)
-            def _():
-                hop(k, 1, p, x_send, c_recv, sibling).wait_send()
-
-                @pl.when(lax.rem(p, GROUP) == 0)
-                def _():
-                    beside(k, 0, lax.div(p, GROUP)).wait_send()
-
-        loop(0, 4 * PIECES, drain)
+            hop(k, 1, p, x_send, c_recv, sibling).wait_send()
+
+            @pl.when(lax.rem(p, GROUP) == 0)
+            def _():
+                beside(k, 0, lax.div(p, GROUP)).wait_send()
+
+        loop(0, 2 * PIECES, drain)
+        for i in range(3):
+            handed(i).wait_send()
+        back.wait()
 
     @pl.when(second)
     def _():
         pl.semaphore_wait(go_sem, 1)
         stage0(0)
+        for i in (1, 2):
+            handed(i).wait_recv()
         stage0(1)
 
+        def pass_on(k):
+            for p in range(PIECES):
+                hop(k, 1, p, c_send, c_recv, down).start()
+                hop(k, 0, p, x_send, c_recv, 2).start()
+
         def early_turn(m):
-            plane_turn(m, 0, 4)
-
-            @pl.when(m == 3)
-            def _():
-                fetch.wait()
+            plane_turn(m, 0, SLOTS)
 
             @pl.when(m >= 3)
             def _():
                 q = m - 3
                 final(q)
 
-                @pl.when(q < 3)
-                def _():
-                    loop(q * PIECES, (q + 1) * PIECES, lambda j: relay(j, False))
-                    from_sibling(q)
-                    convert(solved.at[q])
+                @pl.when((q == 0) | (q == 2))
+                def _():
+                    k = lax.div(q, 2)
+                    loop(k * PIECES, (k + 1) * PIECES, lambda j: relay(j, False))
+                    from_sibling(k)
+
+                @pl.when(q == 0)
+                def _():
+                    fetch.wait()
+
+                @pl.when(q == 1)
+                def _():
+                    handed(0).wait_recv()
+
+                @pl.when(q == 6)
+                def _():
+                    convert(out_panel(0))
+
+                @pl.when((q != 1) & (q != 6))
+                def _():
+                    convert(solved.at[jnp.where(q == 0, 0, jnp.where((q == 2) | (q == 4), 1, 2))])
+
+                unfold(q)
+
+                @pl.when((q == 0) | (q == 4) | (q == 5))
+                def _():
+                    subtract_all(0)
+
+                @pl.when((q == 1) | (q == 2))
+                def _():
+                    subtract_ahead(2)
 
                 @pl.when(q == 3)
                 def _():
-                    convert(out_panel(0))
+                    assign_ahead(2)
+                    pass_on(2)
+                    handed(3).start()
+
+                @pl.when(q == 6)
+                def _():
+                    assign_all(0, 3)
+                    pass_on(3)
+
+        loop(0, EARLY + 3, early_turn)
+        def turn(m):
+            plane_turn(m, 0, SLOTS)
+
+            @pl.when(m >= EARLY + 3)
+            def _():
+                q = m - 3
+                j = q - EARLY
+                final(q)
+
+                @pl.when(lax.rem(j, 2) == 0)
+                def _():
+                    convert(solved.at[lax.div(j, 2)])
 
                 unfold(q)
-
-                @pl.when(q == 3)
-                def _():
-                    assign_all(0, 3)
-                    for p in range(PIECES):
-                        hop(3, 1, p, c_send, c_recv, down).start()
-                        hop(3, 0, p, x_send, c_recv, sibling).start()
-
-                @pl.when(q != 3)
-                def _():
-                    subtract_all(0)
-
-        loop(0, 7, early_turn)
-        stage0(4)
-        stage0(5)
-
-        def turn(m):
-            plane_turn(m, 4, UNITS)
-
-            @pl.when(m >= 7)
-            def _():
-                q = m - 3
-                final(q)
-
-                @pl.when(q % 2 == 0)
-                def _():
-                    convert(solved.at[(q - 4) // 2])
-
-                unfold(q)
-                subtract_all(1 + q % 2)
-
-        loop(4, UNITS + 3, turn)
-        drain_shares(UNITS)
-        loop(0, 4 * PIECES, lambda j: hop(j // PIECES, 1, j % PIECES, c_send, c_recv, down).wait_send())
-        loop(0, PIECES, lambda p: hop(3, 0, p, x_send, c_recv, sibling).wait_send())
+                subtract_all(1 + lax.rem(j, 2))
+
+        loop(EARLY + 3, SLOTS + 3, turn)
+        drain_shares(SLOTS)
+        loop(0, 4 * PIECES, lambda j: hop(lax.div(j, PIECES), 1, lax.rem(j, PIECES), c_send, c_recv, down).wait_send())
+        loop(2 * PIECES, 4 * PIECES, lambda j: hop(lax.div(j, PIECES), 0, lax.rem(j, PIECES), x_send, c_recv, 2).wait_send())
+        handed(3).wait_send()
 
 
     @pl.when(row > 1)
@@ -557,20 +620,22 @@
         in_specs=[pl.BlockSpec(memory_space=pl.ANY)] * 3,
         out_specs=pl.BlockSpec(memory_space=pltpu.VMEM),
         scratch_shapes=[
-            pltpu.VMEM((UNITS, panel, panel), F32),
+            pltpu.VMEM((SLOTS, panel, panel), F32),
             pltpu.VMEM((count, panel, width), F32),
             pltpu.VMEM((3 * panel, width), BF16),
             pltpu.VMEM((panel, 3 * panel), BF16),
             pltpu.SemaphoreType.REGULAR,
             sem((1,)),
-            sem((UNITS,)),
-            sem((UNITS, 2, 16)),
-            sem((UNITS, 26)),
+            sem((SLOTS,)),
+            sem((SLOTS, 2, 16)),
+            sem((SLOTS, 26)),
             sem((count, PIECES)),
             sem((count, PIECES)),
             sem((count, PIECES // GROUP)),
             sem((count, PIECES // GROUP)),
             sem((count, PIECES)),
+            sem((4,)),
+            sem((4,)),
         ],
         compiler_params=pltpu.CompilerParams(
             collective_id=0, has_side_effects=True, vmem_limit_bytes=62_200_000

time: 115 us -> 110 us (0.957); the launches traced: 113 us -> 110 us
  Pallas kernels: 111 us -> 107 us
    pallas_call x1, Pallas kernels: 111 us -> 107 us  [per_device(): pl.pallas_call(kernel, out_shape=pltpu.VMEM((rows, width), F32), in_specs...]
where the time goes in v3:
time: 110 us
  Pallas kernels  107 us (97%)
  local copies, waits for them, and re-layouts  2.19 us (2%)
    pallas_call x1, Pallas kernels, per_device(): pl.pallas_call(kernel, out_shape=pltpu.VMEM((rows, width), F32), in_specs...  107 us

profile of v3, /device:TPU:32, one launch (start us, length us, event | category | flops | bytes accessed | tf_op | source)
XLA Modules:
  0.0 109.5 jit_solution(11017774284261879762)
XLA Ops:
  0.0 107.3 %forward_substitution.1 = f32[1536,768]{1,0:T(8,128)S(1)} custom-call(f32[1536,768]{1,0:T(8,128)} %rhs.1, f32[4,32,1536]{2,1,0:T(8,128)} %bitcast.2, f32[4,32,512]{2,1,0:T(8,128)} %bitcast.3), custom_call_target="tpu_custom_call" | custom-call | tf_op jit(solution)/shard_map/forward_substitution/pallas_call | solution.py:617
  107.3 2.2 %copy.5 = f32[1536,768]{1,0:T(8,128)} copy(f32[1536,768]{1,0:T(8,128)S(1)} %forward_substitution.1) | data formatting | bytes 9437184

commit v4 on v3

--- a/solution.py
+++ b/solution.py
@@ -16,7 +16,7 @@
 PIECES = 16
 GROUP = 4
 SPOTS = 8
-S_FIRST, S_HOP, S_NUM, S_DEN = 32, 4, 5, 4
+S_FIRST, S_HOP, S_NUM, S_DEN = 32, 5, 5, 4
 GO = 1
 LAG = -(-(S_FIRST + 7 * S_HOP + 16) // 4)
 SLACK = 11
@@ -234,6 +234,33 @@
         out[to, cols] = acc
         solved[k, :, cols] = acc
 
+
+    half3 = 3 * half_panel
+
+    def convert_half(k, which, turn):
+        def body(b, _):
+            start = pl.multiple_of(b * 32, 32)
+            high, low = split(solved[k, pl.ds(pl.multiple_of(which * half_panel + start, 32), 32), :])
+            for i, v in enumerate((high, low, high)):
+                right3[pl.ds(pl.multiple_of(turn * half3 + i * half_panel + start, 32), 32), :] = v
+            return 0
+
+        lax.fori_loop(0, half_panel // 32, body, 0)
+
+    def unfold_half(unit, which):
+        for b in range(half_panel // 128):
+            start = pl.multiple_of(which * half_panel + b * 128, 128)
+            for g in range(panel // 128):
+                high, low = split(share[unit, pl.ds(start, 128), g * 128 : (g + 1) * 128].T)
+                for i, v in enumerate((high, high, low)):
+                    left3[g * 128 : (g + 1) * 128, i * half_panel + b * 128 : i * half_panel + (b + 1) * 128] = v
+
+    def subtract_half(block, dest, turn):
+        cols = pl.ds(block * 256, 256)
+        to = pl.ds(pl.multiple_of(dest * panel, panel), panel)
+        acc = jnp.dot(left3[:, :half3], right3[turn * half3 : (turn + 1) * half3, cols], preferred_element_type=F32)
+        out[to, cols] = out[to, cols] - acc
+
     def subtract_ahead(k):
         def body(block, _):
             cols, _, acc = product(block, 0)
@@ -278,7 +305,6 @@
         lax.fori_loop(first, last, turn, 0)
 
     fetch = pltpu.make_async_copy(rhs, out, io_sem.at[0])
-    fetch.start()
 
     def mine(t):
         return share.at[t, pl.ds(pl.multiple_of(col * slab, slab), slab), :]
@@ -338,6 +364,7 @@
     def _():
         loop(3, SLOTS, lambda t: take_inverse(t, 0).wait())
 
+    fetch.start()
     pl.semaphore_wait(barrier, jnp.where((row == 1) | (row == 2), 8, 7))
 
 
@@ -445,6 +472,7 @@
             def _():
                 q = m - 3
                 final(q)
+                unfold(q)
 
                 @pl.when((q == 0) | (q == 2))
                 def _():
@@ -467,8 +495,6 @@
                 @pl.when((q != 1) & (q != 6))
                 def _():
                     convert(solved.at[jnp.where(q == 0, 0, jnp.where((q == 2) | (q == 4), 1, 2))])
-
-                unfold(q)
 
                 @pl.when((q == 0) | (q == 4) | (q == 5))
                 def _():
@@ -515,15 +541,19 @@
 
     @pl.when(row > 1)
     def _():
-        farthest = jnp.maximum(hops, 8 - hops)
-        lag = lax.div(S_FIRST + S_HOP * farthest + 16 + 3, 4)
+        near = hops <= 4
+        halves = (jnp.where(near, core, 1 - core), jnp.where(near, 1 - core, core))
+        lags = [
+            lax.div(S_FIRST + S_HOP * h + 16 + 3, 4)
+            for h in (jnp.minimum(hops, 8 - hops), jnp.maximum(hops, 8 - hops))
+        ]
         due = S_FIRST + S_HOP * hops
 
         def relayed(spot):
             ahead = jnp.maximum(spot - due, 0)
             return jnp.minimum(lax.div(ahead * S_NUM, S_DEN), 4 * PIECES)
 
-        def taken(slot):
+        def taken(slot, lag):
             ready = jnp.minimum(slot - lag + 1, lax.div(jnp.maximum(slot - SLACK + 2, 0), 2))
             return jnp.clip(ready, 0, UNITS)
 
@@ -531,7 +561,7 @@
         stage0(1)
 
         def tile_turn(m, e, carry):
-            before, done = carry
+            before, done = list(carry[:2]), carry[2]
             for i in range(SPOTS):
                 if i == 0:
 
@@ -559,41 +589,44 @@
                 loop(done, now, lambda j: relay(j, True))
                 done = now
 
-                part = i % 4
-                if part == 0:
-                    after = taken(2 * m + i // 4)
+                turn = (i % 4) // 2
+                if i % 2 == 0:
+                    after = taken(2 * m + i // 4, lags[turn])
                     q = after - 1
                     k, u = lax.div(jnp.maximum(q, 0), 3), lax.rem(jnp.maximum(q, 0), 3)
-                    fresh = after > before
-                    before = after
+                    fresh = after > before[turn]
+                    before[turn] = after
 
                     @pl.when(fresh)
                     def _():
-                        final(q)
-
-                        @pl.when(q == 0)
-                        def _():
-                            fetch.wait()
+                        if turn == 0:
+                            final(q)
+
+                            @pl.when(q == 0)
+                            def _():
+                                fetch.wait()
 
                         @pl.when(u == 0)
                         def _():
-                            from_sibling(k)
-                            convert(solved.at[k])
-
-                        unfold(q)
+                            pl.when(near if turn == 1 else jnp.logical_not(near))(lambda: from_sibling(k))
+                            convert_half(k, halves[turn], turn)
+
+                        unfold_half(q, halves[turn])
+                        subtract_half(0, u, turn)
                 else:
 
                     @pl.when(fresh)
                     def _():
-                        subtract(part - 1, u)
-
-            return before, done
+                        subtract_half(1, u, turn)
+                        subtract_half(2, u, turn)
+
+            return before[0], before[1], done
 
         def turn(t, carry):
             carry = tile_turn(2 * t, 1, carry)
             return tile_turn(2 * t + 1, -1, carry)
 
-        lax.fori_loop(0, TURNS, turn, (jnp.int32(0), jnp.int32(0)))
+        lax.fori_loop(0, TURNS, turn, (jnp.int32(0),) * 3)
         drain_shares(UNITS)
 
         def drain(j):

time: 110 us -> 106 us (0.964)
  Pallas kernels: 107 us -> 104 us
    pallas_call x1, Pallas kernels: 107 us -> 104 us  [per_device(): pl.pallas_call(kernel, out_shape=pltpu.VMEM((rows, width), F32), in_specs...]
where the time goes in v4:
time: 106 us
  Pallas kernels  104 us (98%)
  local copies, waits for them, and re-layouts  2.19 us (2%)
    pallas_call x1, Pallas kernels, per_device(): pl.pallas_call(kernel, out_shape=pltpu.VMEM((rows, width), F32), in_specs...  104 us
    unnamed x1, local copies, waits for them, and re-layouts  2.19 us

profile of v4, /device:TPU:32, one launch (start us, length us, event | category | flops | bytes accessed | tf_op | source)
XLA Modules:
  0.0 105.7 jit_solution(12404318644722431074)
XLA Ops:
  0.0 103.5 %forward_substitution.1 = f32[1536,768]{1,0:T(8,128)S(1)} custom-call(f32[1536,768]{1,0:T(8,128)} %rhs.1, f32[4,32,1536]{2,1,0:T(8,128)} %bitcast.2, f32[4,32,512]{2,1,0:T(8,128)} %bitcast.3), custom_call_target="tpu_custom_call" | custom-call | tf_op jit(solution)/shard_map/forward_substitution/pallas_call | solution.py:650
  103.5 2.2 %copy.5 = f32[1536,768]{1,0:T(8,128)} copy(f32[1536,768]{1,0:T(8,128)S(1)} %forward_substitution.1) | data formatting | bytes 9437184

commit v5 on v4

--- a/solution.py
+++ b/solution.py
@@ -305,6 +305,7 @@
         lax.fori_loop(first, last, turn, 0)
 
     fetch = pltpu.make_async_copy(rhs, out, io_sem.at[0])
+    fetch.start()
 
     def mine(t):
         return share.at[t, pl.ds(pl.multiple_of(col * slab, slab), slab), :]
@@ -364,7 +365,6 @@
     def _():
         loop(3, SLOTS, lambda t: take_inverse(t, 0).wait())
 
-    fetch.start()
     pl.semaphore_wait(barrier, jnp.where((row == 1) | (row == 2), 8, 7))
 
 
@@ -472,7 +472,6 @@
             def _():
                 q = m - 3
                 final(q)
-                unfold(q)
 
                 @pl.when((q == 0) | (q == 2))
                 def _():
@@ -495,6 +494,8 @@
                 @pl.when((q != 1) & (q != 6))
                 def _():
                     convert(solved.at[jnp.where(q == 0, 0, jnp.where((q == 2) | (q == 4), 1, 2))])
+
+                unfold(q)
 
                 @pl.when((q == 0) | (q == 4) | (q == 5))
                 def _():

time: 106 us -> 105 us (level)
  no operation moved by 1% of the time
where the time goes in v5:
time: 105 us
  Pallas kernels  103 us (98%)
  local copies, waits for them, and re-layouts  2.19 us (2%)
    pallas_call x1, Pallas kernels, per_device(): pl.pallas_call(kernel, out_shape=pltpu.VMEM((rows, width), F32), in_specs...  103 us
    unnamed x1, local copies, waits for them, and re-layouts  2.19 us

profile of v5, /device:TPU:32, one launch (start us, length us, event | category | flops | bytes accessed | tf_op | source)
XLA Modules:
  0.0 105.0 jit_solution(6538127147693496899)
XLA Ops:
  0.0 102.8 %forward_substitution.1 = f32[1536,768]{1,0:T(8,128)S(1)} custom-call(f32[1536,768]{1,0:T(8,128)} %rhs.1, f32[4,32,1536]{2,1,0:T(8,128)} %bitcast.2, f32[4,32,512]{2,1,0:T(8,128)} %bitcast.3), custom_call_target="tpu_custom_call" | custom-call | tf_op jit(solution)/shard_map/forward_substitution/pallas_call | solution.py:651
  102.8 2.2 %copy.5 = f32[1536,768]{1,0:T(8,128)} copy(f32[1536,768]{1,0:T(8,128)S(1)} %forward_substitution.1) | data formatting | bytes 9437184
